TPU v7x, 32 devices: a whole 2x2x4 slice. The times are simulated.
32 devices in a mesh: ctx: 8 (over z, y), dp: 4 (over x, core).
Axes of the slice: x: 2, y: 2, z: 4, core: 2. Of those that a mesh axis runs over, the one named last changes fastest.
Arguments:
- tokens: bfloat16 [8, 512, 4096], P('dp', 'ctx'), may hold values from -6 to 6
- queries: bfloat16 [8, 512, 2048], P('dp', 'ctx'), may hold values from -160 to 160
- d_attended: bfloat16 [8, 512, 2048], P('dp', 'ctx'), may hold values from -6 to 6
- span_order: int32 [16], replicated, may hold values from 0 to 15, each once
- norm_gain: float32 [4096], replicated, may hold values from 0.1 to 1.9
- key_weight: bfloat16 [4096, 512], replicated, may hold values from -0.09375 to 0.09375
- value_weight: bfloat16 [4096, 512], replicated, may hold values from -0.09375 to 0.09375
Outputs:
- attended: bfloat16 [8, 512, 2048], P('dp', 'ctx')
- grad_queries: bfloat16 [8, 512, 2048], P('dp', 'ctx')
- grad_tokens: bfloat16 [8, 512, 4096], P('dp', 'ctx')
- grad_key_weight: float32 [4096, 512], P(('ctx', 'dp'))
- grad_value_weight: float32 [4096, 512], P(('ctx', 'dp'))
- grad_gain: float32 [4096], P(('ctx', 'dp'))
All inputs are finite; a program needn't handle non-finite values.
Results may differ from a plain program's by a relative error of at most 0.025.
The roundings to bfloat16 on the way count: a program that leaves them out, or rounds other values in their place, can miss the bound.
Values may be sent and summed in bfloat16 or wider, within the bound.
No kernel may reach another device: no remote copies, remote signals or barrier semaphores. Data moves between devices by JAX's collectives and lax.ppermute only.
A program may use at most 192 MiB of HBM per device.

v0:
```python
import jax
import jax.numpy as jnp
from jax import lax
from jax.sharding import PartitionSpec as P

KV_HEADS = 4
HEAD_DIM = 128


ROPE_BASE = 500000.0
EPSILON = 1e-05


def positions(span_order, span_len):
    offsets = jnp.arange(span_len, dtype=jnp.int32)
    return (span_order[:, None] * span_len + offsets[None, :]).reshape(-1)


def rotation(token_pos, head_size):
    half_dim = head_size // 2
    frequency = ROPE_BASE ** (-2.0 * jnp.arange(half_dim, dtype=jnp.float32) / head_size)
    angles = token_pos.astype(jnp.float32)[:, None] * frequency[None, :]
    angles = jnp.concatenate([angles, angles], axis=1)
    return (jnp.cos(angles), jnp.sin(angles))


def rotate_half(values):
    half_dim = values.shape[-1] // 2
    return jnp.concatenate([-values[..., half_dim:], values[..., :half_dim]], axis=-1)


def rotate_back(values):
    half_dim = values.shape[-1] // 2
    return jnp.concatenate([values[..., half_dim:], -values[..., :half_dim]], axis=-1)


def normalize(tokens, norm_gain):
    widened = tokens.astype(jnp.float32)
    rms_scale = lax.rsqrt(jnp.mean(widened * widened, axis=-1, keepdims=True) + EPSILON)
    return ((widened * rms_scale * norm_gain).astype(jnp.bfloat16), rms_scale)


def project_keys(normed, key_weight, value_weight, cosine, sine_table, kv_heads, head_size):
    row_count = normed.shape[0]
    key_pre = jnp.dot(normed, key_weight, preferred_element_type=jnp.float32).reshape(
        row_count, kv_heads, head_size
    )
    rotated = key_pre * cosine[:, None, :] + rotate_half(key_pre) * sine_table[:, None, :]
    value_rows = jnp.dot(normed, value_weight, preferred_element_type=jnp.float32)
    return (
        rotated.reshape(row_count, kv_heads * head_size).astype(jnp.bfloat16),
        value_rows.astype(jnp.bfloat16),
    )


def attend_group(query_group, grad_group, key_group, value_group, causal_mask, score_scale):
    scores = (
        jnp.einsum("tgd,sd->gts", query_group, key_group, preferred_element_type=jnp.float32)
        * score_scale
    )
    scores = jnp.where(causal_mask[None], scores, -1e30)
    row_max = jnp.max(scores, axis=-1, keepdims=True)
    exponent = jnp.exp(scores - row_max)
    probability = exponent / jnp.sum(exponent, axis=-1, keepdims=True)
    probability_b = probability.astype(jnp.bfloat16)
    attended = jnp.einsum(
        "gts,sd->tgd", probability_b, value_group, preferred_element_type=jnp.float32
    ).astype(jnp.bfloat16)
    dprob = jnp.einsum("tgd,sd->gts", grad_group, value_group, preferred_element_type=jnp.float32)
    delta = jnp.sum(grad_group.astype(jnp.float32) * attended.astype(jnp.float32), axis=-1)
    dscores = (probability * (dprob - jnp.transpose(delta)[:, :, None])).astype(jnp.bfloat16)
    dquery = (
        jnp.einsum("gts,sd->tgd", dscores, key_group, preferred_element_type=jnp.float32)
        * score_scale
    ).astype(jnp.bfloat16)
    key_term = (
        jnp.einsum("gts,tgd->sd", dscores, query_group, preferred_element_type=jnp.float32)
        * score_scale
    )
    value_term = jnp.einsum(
        "gts,tgd->sd", probability_b, grad_group, preferred_element_type=jnp.float32
    )
    return (attended, dquery, key_term, value_term)


def attend_device(queries, grads, all_keys, all_values, query_pos, key_pos, kv_heads, head_size):
    row_count = queries.shape[0]
    group_size = queries.shape[1] // (kv_heads * head_size)
    group_width = group_size * head_size
    causal_mask = key_pos[None, :] <= query_pos[:, None]
    score_scale = head_size ** (-0.5)
    outputs = []
    for head_group in range(kv_heads):
        query_group = queries[:, head_group * group_width : (head_group + 1) * group_width].reshape(
            row_count, group_size, head_size
        )
        grad_group = grads[:, head_group * group_width : (head_group + 1) * group_width].reshape(
            row_count, group_size, head_size
        )
        key_group = all_keys[:, head_group * head_size : (head_group + 1) * head_size]
        value_group = all_values[:, head_group * head_size : (head_group + 1) * head_size]
        outputs.append(
            attend_group(query_group, grad_group, key_group, value_group, causal_mask, score_scale)
        )
    attended = jnp.concatenate(
        [item[0].reshape(row_count, group_width) for item in outputs], axis=1
    )
    dquery = jnp.concatenate([item[1].reshape(row_count, group_width) for item in outputs], axis=1)
    key_terms = jnp.concatenate([item[2] for item in outputs], axis=1)
    value_terms = jnp.concatenate([item[3] for item in outputs], axis=1)
    return (attended, dquery, key_terms, value_terms)


def finish_backward(
    tokens,
    normed,
    rms_scale,
    key_grad,
    value_grad,
    cosine,
    sine_table,
    norm_gain,
    key_weight,
    value_weight,
    kv_heads,
    head_size,
):
    row_count = tokens.shape[0]
    shaped = key_grad.reshape(row_count, kv_heads, head_size)
    key_pre_grad = (
        (shaped * cosine[:, None, :] + rotate_back(shaped * sine_table[:, None, :]))
        .reshape(row_count, kv_heads * head_size)
        .astype(jnp.bfloat16)
    )
    value_pre_grad = value_grad.astype(jnp.bfloat16)
    weight_key = jnp.dot(normed.T, key_pre_grad, preferred_element_type=jnp.float32)
    weight_value = jnp.dot(normed.T, value_pre_grad, preferred_element_type=jnp.float32)
    normed_grad = jnp.dot(key_pre_grad, key_weight.T, preferred_element_type=jnp.float32) + jnp.dot(
        value_pre_grad, value_weight.T, preferred_element_type=jnp.float32
    )
    widened = tokens.astype(jnp.float32)
    gain_part = jnp.sum(normed_grad * widened * rms_scale, axis=0)
    inner_mean = jnp.mean(normed_grad * norm_gain * widened, axis=-1, keepdims=True)
    grad_rows = (
        rms_scale * norm_gain * normed_grad - widened * rms_scale**3 * inner_mean
    ).astype(jnp.bfloat16)
    return (grad_rows, weight_key, weight_value, gain_part)


def body(tokens, queries, d_attended, span_order, norm_gain, key_weight, value_weight):
    local_seqs = tokens.shape[0]
    row_count = tokens.shape[1]
    model_width = tokens.shape[2]
    kv_width = key_weight.shape[1]
    shard_index = lax.axis_index("ctx")
    token_pos = positions(span_order, row_count // 2)
    query_pos = lax.dynamic_slice_in_dim(token_pos, shard_index * row_count, row_count, 0)
    cosine, sine_table = rotation(query_pos, HEAD_DIM)
    cosine_all = jnp.tile(cosine, (local_seqs, 1))
    sine_all = jnp.tile(sine_table, (local_seqs, 1))
    flat_tokens = tokens.reshape(local_seqs * row_count, model_width)
    normed, rms_scale = normalize(flat_tokens, norm_gain)
    rotated_keys, value_rows = project_keys(
        normed, key_weight, value_weight, cosine_all, sine_all, KV_HEADS, HEAD_DIM
    )
    rotated_keys = rotated_keys.reshape(local_seqs, row_count, kv_width)
    value_rows = value_rows.reshape(local_seqs, row_count, kv_width)
    all_keys, all_values = (
        lax.all_gather(rotated_keys, "ctx", axis=1, tiled=True),
        lax.all_gather(value_rows, "ctx", axis=1, tiled=True),
    )
    attended_list, dquery_list, key_list, value_list = ([], [], [], [])
    for sequence in range(local_seqs):
        attended, dquery, key_terms, value_terms = attend_device(
            queries[sequence],
            d_attended[sequence],
            all_keys[sequence],
            all_values[sequence],
            query_pos,
            token_pos,
            KV_HEADS,
            HEAD_DIM,
        )
        attended_list.append(attended)
        dquery_list.append(dquery)
        key_list.append(key_terms)
        value_list.append(value_terms)
    key_stack = jnp.stack(key_list)
    value_stack = jnp.stack(value_list)
    key_grad, value_grad = (
        lax.psum_scatter(
            key_stack.astype(jnp.bfloat16), "ctx", scatter_dimension=1, tiled=True
        ).astype(jnp.float32),
        lax.psum_scatter(
            value_stack.astype(jnp.bfloat16), "ctx", scatter_dimension=1, tiled=True
        ).astype(jnp.float32),
    )
    key_grad = key_grad.reshape(local_seqs * row_count, kv_width)
    value_grad = value_grad.reshape(local_seqs * row_count, kv_width)
    grad_rows, weight_key, weight_value, gain_part = finish_backward(
        flat_tokens,
        normed,
        rms_scale,
        key_grad,
        value_grad,
        cosine_all,
        sine_all,
        norm_gain,
        key_weight,
        value_weight,
        KV_HEADS,
        HEAD_DIM,
    )
    weight_key, weight_value, gain_part = (
        lax.psum_scatter(
            weight_key.astype(jnp.bfloat16), "ctx", scatter_dimension=0, tiled=True
        ).astype(jnp.float32),
        lax.psum_scatter(
            weight_value.astype(jnp.bfloat16), "ctx", scatter_dimension=0, tiled=True
        ).astype(jnp.float32),
        lax.psum_scatter(
            gain_part.astype(jnp.bfloat16), "ctx", scatter_dimension=0, tiled=True
        ).astype(jnp.float32),
    )
    weight_key, weight_value, gain_part = (
        lax.psum_scatter(
            weight_key.astype(jnp.bfloat16), "dp", scatter_dimension=0, tiled=True
        ).astype(jnp.float32),
        lax.psum_scatter(
            weight_value.astype(jnp.bfloat16), "dp", scatter_dimension=0, tiled=True
        ).astype(jnp.float32),
        lax.psum_scatter(
            gain_part.astype(jnp.bfloat16), "dp", scatter_dimension=0, tiled=True
        ).astype(jnp.float32),
    )
    return (
        jnp.stack(attended_list),
        jnp.stack(dquery_list),
        grad_rows.reshape(local_seqs, row_count, model_width),
        weight_key,
        weight_value,
        gain_part,
    )


def solution(mesh):
    placed = (P("dp", "ctx", None), P("dp", "ctx", None), P("dp", "ctx", None), P(), P(), P(), P())
    return jax.shard_map(
        body,
        mesh=mesh,
        in_specs=placed,
        out_specs=(
            P("dp", "ctx", None),
            P("dp", "ctx", None),
            P("dp", "ctx", None),
            P(("ctx", "dp"), None),
            P(("ctx", "dp"), None),
            P(("ctx", "dp")),
        ),
        check_vma=False,
    )
```

profile of v0, /device:TPU:0, one launch (start us, length us, event | category | flops | bytes accessed | tf_op | source)
XLA Modules:
  0.0 512.8 jit_solution(5786807104449921285)
XLA Ops:
  10.2 6.5 %copy.154 = bf16[512,4096]{1,0:T(8,128)(2,1)} copy(bf16[512,4096]{0,1:T(8,128)(2,1)} %bitcast.753) | data formatting | bytes 8388608 | tf_op jit(solution)/shard_map/dot_general | solution.py:45
  17.0 3.4 fusion.276
  21.9 3.7 convolution_convert_fusion.1
  27.7 36.9 %all-gather.5.cloned.1.call-done = bf16[2,512,512]{2,1,0:T(8,128)(2,1)} async-done(((bf16[2,64,512]{2,1,0:T(8,128)(2,1)}), bf16[2,512,512]{2,1,0:T(8,128)(2,1)}) %all-gather.5.cloned.1.call-update) | async-done | bytes 1048592 | tf_op jit(solution)/shard_map/all_gather | solution.py:169
  65.9 1.7 fusion.264
  68.8 1.7 fusion.94
  70.5 35.8 %all-gather.3.cloned.1.call-done = bf16[2,512,512]{2,1,0:T(8,128)(2,1)} async-done(((bf16[2,64,512]{2,1,0:T(8,128)(2,1)}), bf16[2,512,512]{2,1,0:T(8,128)(2,1)}) %all-gather.3.cloned.1.call-update) | async-done | bytes 1048592 | tf_op jit(solution)/shard_map/all_gather | solution.py:170
  106.3 2.1 slice_bitcast_fusion.3
  109.8 2.0 fusion.267
  113.6 2.4 multiply_reduce_fusion.5
  116.8 2.0 fusion.270
  120.6 2.4 multiply_reduce_fusion.6
  123.9 2.4 fusion.273
  127.5 2.4 multiply_reduce_fusion.7
  130.8 2.5 fusion.252
  136.8 2.5 fusion.255
  142.8 2.4 fusion.258
  148.8 1.9 fusion.261
  163.6 2.1 copy.150
  168.1 2.1 copy.137
  172.1 99.3 %all-reduce.7.cloned.1.call-done = (bf16[2,512,512]{2,0,1:T(2,128)(2,1)}, bf16[2,512,512]{2,0,1:T(2,128)(2,1)}) async-done(((bf16[2,512,512]{2,0,1:T(2,128)(2,1)}, bf16[2,512,512]{2,0,1:T(2,128)(2,1)}), (bf16[2,512,512]{2,0,1:T(2,128)(2,1)}, bf16[2,512,512]{2,0,1:T(2,128)(2,1)})) %all-reduce.7.cloned.1.call-update) | async-done | bytes 2097168
  273.4 3.2 convolution_convert_fusion
  277.8 3.3 bitcast_convert_fusion
  283.7 1.8 copy.139
  295.8 68.7 %reduce-scatter.5.cloned.1.call-done = bf16[512,512]{1,0:T(8,128)(2,1)} async-done(((bf16[4096,512]{1,0:T(8,128)(2,1)}), bf16[512,512]{1,0:T(8,128)(2,1)}) %reduce-scatter.5.cloned.1.call-update) | async-done | bytes 524304 | tf_op jit(solution)/shard_map/reduce_scatter | solution.py:215
  364.6 3.8 fusion.277
  368.5 1.7 fusion.18
  370.2 21.3 %all-reduce.2 = bf16[4096]{0:T(1024)(128)(2,1)S(1)} all-reduce(bf16[4096]{0:T(1024)(128)(2,1)S(1)} %get-tuple-element.6), channel_id=8, replica_groups=mesh['ctx'=8,'dp'=4] {'ctx'}, use_global_device_ids=true, to_apply=%region_33.34.clone | all-reduce | flops 4096 | bytes 16384
  391.6 6.0 %all-reduce.3 = bf16[512]{0:T(512)(128)(2,1)S(1)} all-reduce(bf16[512]{0:T(512)(128)(2,1)S(1)} %dynamic-slice.5), channel_id=9, replica_groups=mesh['ctx'=8,'dp'=4] {'dp'}, use_global_device_ids=true, to_apply=%region_34.35.clone | all-reduce | flops 512 | bytes 2048
  397.7 58.8 %reduce-scatter.9.cloned.1.call-done = bf16[512,512]{1,0:T(8,128)(2,1)} async-done(((bf16[4096,512]{1,0:T(8,128)(2,1)}), bf16[512,512]{1,0:T(8,128)(2,1)}) %reduce-scatter.9.cloned.1.call-update) | async-done | bytes 524304 | tf_op jit(solution)/shard_map/reduce_scatter | solution.py:218
  458.7 21.4 %reduce-scatter.7.cloned.1.call-done = bf16[128,512]{1,0:T(8,128)(2,1)} async-done(((bf16[512,512]{1,0:T(8,128)(2,1)}), bf16[128,512]{1,0:T(8,128)(2,1)}) %reduce-scatter.7.cloned.1.call-update) | async-done | bytes 131088 | tf_op jit(solution)/shard_map/reduce_scatter | solution.py:226
  481.7 22.5 %reduce-scatter.11.cloned.1.call-done = bf16[128,512]{1,0:T(8,128)(2,1)} async-done(((bf16[512,512]{1,0:T(8,128)(2,1)}), bf16[128,512]{1,0:T(8,128)(2,1)}) %reduce-scatter.11.cloned.1.call-update) | async-done | bytes 131088 | tf_op jit(solution)/shard_map/reduce_scatter | solution.py:229
  (335 shorter events, 64.2 us)
Async XLA Ops:
  7.2 57.4 %all-gather.5.cloned.1.call-start = ((), (), s32[]{:S(2)}) async-start(), calls=%async_computation.5 | async-start | bytes 1179648 | tf_op jit(solution)/shard_map/all_gather | solution.py:169
  10.2 6.5 %copy-start = (bf16[2,64,4096]{2,1,0:T(8,128)(2,1)S(1)}, bf16[2,64,4096]{2,1,0:T(8,128)(2,1)}, u32[]{:S(2)}) copy-start(bf16[2,64,4096]{2,1,0:T(8,128)(2,1)} %param.7) | copy-start | bytes 3145732
  10.2 6.5 %copy-start.56 = (f32[4096]{0:T(1024)S(1)}, f32[4096]{0:T(1024)}, u32[]{:S(2)}) copy-start(f32[4096]{0:T(1024)} %param.11) | copy-start | bytes 49156
  21.4 84.9 %all-gather.3.cloned.1.call-start = ((), (), s32[]{:S(2)}) async-start(), calls=%async_computation.4 | async-start | bytes 1179648 | tf_op jit(solution)/shard_map/all_gather | solution.py:170
  25.6 245.8 %all-reduce.7.cloned.1.call-start = ((), (), s32[]{:S(2)}) async-start(), calls=%async_computation.10 | async-start | bytes 4194304
  26.7 39.2 %copy-start.69 = (bf16[8,4,8,128]{3,2,1,0:T(8,128)(2,1)}, bf16[8,4,8,128]{3,2,1,0:T(8,128)(2,1)S(1)}, u32[]{:S(2)}) copy-start(bf16[8,4,8,128]{3,2,1,0:T(8,128)(2,1)S(1)} %get-tuple-element.83) | copy-start | bytes 196612
  26.8 39.1 %copy-start.79 = (pred[64,512]{1,0:T(8,128)(4,1)}, pred[64,512]{1,0:T(8,128)(4,1)S(1)}, u32[]{:S(2)}) copy-start(pred[64,512]{1,0:T(8,128)(4,1)S(1)} %broadcast_compare_fusion) | copy-start | bytes 98308
  65.8 58.0 %copy-start.4 = (bf16[512,512]{1,0:T(8,128)(2,1)}, bf16[512,512]{1,0:T(8,128)(2,1)S(1)}, u32[]{:S(2)}) copy-start(bf16[512,512]{1,0:T(8,128)(2,1)S(1)} %get-tuple-element.14) | copy-start | bytes 1572868
  65.8 82.9 %copy-start.2 = (bf16[512,512]{1,0:T(8,128)(2,1)}, bf16[512,512]{1,0:T(8,128)(2,1)S(1)}, u32[]{:S(2)}) copy-start(bf16[512,512]{1,0:T(8,128)(2,1)S(1)} %get-tuple-element.15) | copy-start | bytes 1572868
  111.8 8.8 %copy-start.29 = (bf16[8,4,8,128]{3,2,1,0:T(8,128)(2,1)S(1)}, bf16[8,4,8,128]{3,2,1,0:T(8,128)(2,1)}, u32[]{:S(2)}) copy-start(bf16[8,4,8,128]{3,2,1,0:T(8,128)(2,1)} %get-tuple-element.77) | copy-start | bytes 196612
  113.5 10.3 %copy-start.65 = (bf16[8,4,8,128]{3,2,1,0:T(8,128)(2,1)S(1)}, bf16[8,4,8,128]{3,2,1,0:T(8,128)(2,1)}, u32[]{:S(2)}) copy-start(bf16[8,4,8,128]{3,2,1,0:T(8,128)(2,1)} %get-tuple-element.84) | copy-start | bytes 196612
  118.8 8.7 %copy-start.27 = (bf16[8,4,8,128]{3,2,1,0:T(8,128)(2,1)S(1)}, bf16[8,4,8,128]{3,2,1,0:T(8,128)(2,1)}, u32[]{:S(2)}) copy-start(bf16[8,4,8,128]{3,2,1,0:T(8,128)(2,1)} %get-tuple-element.80) | copy-start | bytes 196612
  120.5 10.2 %copy-start.63 = (bf16[8,4,8,128]{3,2,1,0:T(8,128)(2,1)S(1)}, bf16[8,4,8,128]{3,2,1,0:T(8,128)(2,1)}, u32[]{:S(2)}) copy-start(bf16[8,4,8,128]{3,2,1,0:T(8,128)(2,1)} %get-tuple-element.37) | copy-start | bytes 196612
  126.3 8.1 %copy-start.25 = (bf16[8,4,8,128]{3,2,1,0:T(8,128)(2,1)S(1)}, bf16[8,4,8,128]{3,2,1,0:T(8,128)(2,1)}, u32[]{:S(2)}) copy-start(bf16[8,4,8,128]{3,2,1,0:T(8,128)(2,1)} %get-tuple-element.29) | copy-start | bytes 196612
  126.3 9.1 %copy-start.6 = (bf16[512,512]{1,0:T(8,128)(2,1)S(1)}, bf16[512,512]{1,0:T(8,128)(2,1)}, u32[]{:S(2)}) copy-start(bf16[512,512]{1,0:T(8,128)(2,1)} %get-tuple-element.13) | copy-start | bytes 1572868
  127.5 9.3 %copy-start.61 = (bf16[8,4,8,128]{3,2,1,0:T(8,128)(2,1)S(1)}, bf16[8,4,8,128]{3,2,1,0:T(8,128)(2,1)}, u32[]{:S(2)}) copy-start(bf16[8,4,8,128]{3,2,1,0:T(8,128)(2,1)} %get-tuple-element.38) | copy-start | bytes 196612
  133.2 7.2 %copy-start.23 = (bf16[8,4,8,128]{3,2,1,0:T(8,128)(2,1)S(1)}, bf16[8,4,8,128]{3,2,1,0:T(8,128)(2,1)}, u32[]{:S(2)}) copy-start(bf16[8,4,8,128]{3,2,1,0:T(8,128)(2,1)} %get-tuple-element.30) | copy-start | bytes 196612
  134.4 8.4 %copy-start.59 = (bf16[8,4,8,128]{3,2,1,0:T(8,128)(2,1)S(1)}, bf16[8,4,8,128]{3,2,1,0:T(8,128)(2,1)}, u32[]{:S(2)}) copy-start(bf16[8,4,8,128]{3,2,1,0:T(8,128)(2,1)} %get-tuple-element.39) | copy-start | bytes 196612
  139.3 7.2 %copy-start.21 = (bf16[8,4,8,128]{3,2,1,0:T(8,128)(2,1)S(1)}, bf16[8,4,8,128]{3,2,1,0:T(8,128)(2,1)}, u32[]{:S(2)}) copy-start(bf16[8,4,8,128]{3,2,1,0:T(8,128)(2,1)} %get-tuple-element.31) | copy-start | bytes 196612
  140.4 8.3 %copy-start.57 = (bf16[8,4,8,128]{3,2,1,0:T(8,128)(2,1)S(1)}, bf16[8,4,8,128]{3,2,1,0:T(8,128)(2,1)}, u32[]{:S(2)}) copy-start(bf16[8,4,8,128]{3,2,1,0:T(8,128)(2,1)} %get-tuple-element.36) | copy-start | bytes 196612
  145.2 6.7 %copy-start.20 = (bf16[8,4,8,128]{3,2,1,0:T(8,128)(2,1)S(1)}, bf16[8,4,8,128]{3,2,1,0:T(8,128)(2,1)}, u32[]{:S(2)}) copy-start(bf16[8,4,8,128]{3,2,1,0:T(8,128)(2,1)} %get-tuple-element.28) | copy-start | bytes 196612
  170.2 194.3 %reduce-scatter.5.cloned.1.call-start = ((), (), s32[]{:S(2)}) async-start(), calls=%async_computation.6 | async-start | bytes 4718592 | tf_op jit(solution)/shard_map/reduce_scatter | solution.py:215
  276.7 179.8 %reduce-scatter.9.cloned.1.call-start = ((), (), s32[]{:S(2)}) async-start(), calls=%async_computation.8 | async-start | bytes 4718592 | tf_op jit(solution)/shard_map/reduce_scatter | solution.py:218
  281.1 7.6 %copy-start.3 = (bf16[512,512]{1,0:T(8,128)(2,1)S(1)}, bf16[512,512]{1,0:T(8,128)(2,1)}, u32[]{:S(2)}) copy-start(bf16[512,512]{1,0:T(8,128)(2,1)} %copy-done.2) | copy-start | bytes 1572868
  281.1 199.0 %reduce-scatter.7.cloned.1.call-start = ((), (), s32[]{:S(2)}) async-start(), calls=%async_computation.7 | async-start | bytes 655360 | tf_op jit(solution)/shard_map/reduce_scatter | solution.py:226
  286.9 6.6 %copy-start.71 = (bf16[128,4,64]{0,2,1:T(8,128)(2,1)S(1)}, bf16[128,4,64]{0,2,1:T(8,128)(2,1)}, u32[]{:S(2)}) copy-start(bf16[128,4,64]{0,2,1:T(8,128)(2,1)} %get-tuple-element.69) | copy-start | bytes 196612
  286.9 6.7 %copy-start.72 = (bf16[128,4,64]{0,2,1:T(8,128)(2,1)S(1)}, bf16[128,4,64]{0,2,1:T(8,128)(2,1)}, u32[]{:S(2)}) copy-start(bf16[128,4,64]{0,2,1:T(8,128)(2,1)} %get-tuple-element.71) | copy-start | bytes 196612
  286.9 6.7 %copy-start.73 = (bf16[128,4,64]{0,2,1:T(8,128)(2,1)S(1)}, bf16[128,4,64]{0,2,1:T(8,128)(2,1)}, u32[]{:S(2)}) copy-start(bf16[128,4,64]{0,2,1:T(8,128)(2,1)} %get-tuple-element.73) | copy-start | bytes 196612
  287.2 6.5 %copy-start.75 = (bf16[128,4,64]{0,2,1:T(8,128)(2,1)S(1)}, bf16[128,4,64]{0,2,1:T(8,128)(2,1)}, u32[]{:S(2)}) copy-start(bf16[128,4,64]{0,2,1:T(8,128)(2,1)} %get-tuple-element.61) | copy-start | bytes 196612
  287.2 6.5 %copy-start.77 = (bf16[128,4,64]{0,2,1:T(8,128)(2,1)S(1)}, bf16[128,4,64]{0,2,1:T(8,128)(2,1)}, u32[]{:S(2)}) copy-start(bf16[128,4,64]{0,2,1:T(8,128)(2,1)} %get-tuple-element.65) | copy-start | bytes 196612
  364.6 139.7 %reduce-scatter.11.cloned.1.call-start = ((), (), s32[]{:S(2)}) async-start(), calls=%async_computation.9 | async-start | bytes 655360 | tf_op jit(solution)/shard_map/reduce_scatter | solution.py:229
  368.5 88.6 %copy-start.98 = (f32[128]{0:T(128)S(1)}, f32[128]{0:T(128)}, u32[]{:S(2)}) copy-start(f32[128]{0:T(128)} %multiply_multiply_fusion) | copy-start | bytes 1540
  (76 other events, 205.5 us)
Sparse Core Ops, SparseCore 0:
  21.6 42.9 all-gather.4
  67.3 38.9 all-gather.2
  170.3 101.0 all-reduce.6
  276.8 87.6 reduce-scatter.4
  368.0 88.4 reduce-scatter.8
  458.8 21.2 reduce-scatter.6
  482.6 21.6 reduce-scatter.10
where the time goes:
time: 514 us; the launch traced here: 513 us
  waiting for transfers between devices  344 us (67%)
  matrix products  75.4 us (15%)
  blocking collectives  27.4 us (5%)
  local copies, waits for them, and re-layouts  26.2 us (5%)
  other arithmetic  21.8 us (4%)
  between operations  17.6 us (3%)
    unnamed x8, waiting for transfers between devices  99.4 us
    reduce_scatter x1, waiting for transfers between devices, body(): lax.psum_scatter(weight_key.astype(jnp.bfloat16), 'ctx', scatter_dimensio...  68.7 us
    reduce_scatter x1, waiting for transfers between devices, body(): lax.psum_scatter(weight_value.astype(jnp.bfloat16), 'ctx', scatter_dimens...  58.8 us
    all_gather x1, waiting for transfers between devices, body(): lax.all_gather(rotated_keys, 'ctx', axis=1, tiled=True)  36.9 us
    all_gather x1, waiting for transfers between devices, body(): lax.all_gather(value_rows, 'ctx', axis=1, tiled=True)  35.8 us
    unnamed x2, blocking collectives  27.4 us
    reduce_scatter x1, waiting for transfers between devices, body(): lax.psum_scatter(weight_value.astype(jnp.bfloat16), 'dp', scatter_dimensi...  22.5 us
    reduce_scatter x1, waiting for transfers between devices, body(): lax.psum_scatter(weight_key.astype(jnp.bfloat16), 'dp', scatter_dimension...  21.4 us
  transfers between devices with their start and end apart: 7, of which 7 were waited for; matrix products, arithmetic and copies ran while one was open for 8% of the time, Pallas kernels for 0%

commit v1 on v0

--- a/solution.py
+++ b/solution.py
@@ -1,6 +1,8 @@
 import jax
 import jax.numpy as jnp
 from jax import lax
+from jax.experimental import pallas as pl
+from jax.experimental.pallas import tpu as pltpu
 from jax.sharding import PartitionSpec as P
 
 KV_HEADS = 4
@@ -147,7 +149,7 @@
     return (grad_rows, weight_key, weight_value, gain_part)
 
 
-def body(tokens, queries, d_attended, span_order, norm_gain, key_weight, value_weight):
+def body_rows(tokens, queries, d_attended, span_order, norm_gain, key_weight, value_weight):
     local_seqs = tokens.shape[0]
     row_count = tokens.shape[1]
     model_width = tokens.shape[2]
@@ -243,6 +245,351 @@
     )
 
 
+NT = (((1,), (1,)), ((), ()))
+
+
+def dot32(left, right):
+    return jnp.dot(left, right, preferred_element_type=jnp.float32)
+
+
+def project_kernel(
+    tok_all, tok_part, gain, wk, wv, cosine, sine, normed_out, rms_out, kv_out, acc_k, acc_v, rms_s
+):
+    step = pl.program_id(0)
+    pairs, seq_rows, pair_width = kv_out.shape
+    head = pair_width // 2
+
+    @pl.when(step == 0)
+    def _():
+        wide = tok_all[...].astype(jnp.float32)
+        rms_s[...] = lax.rsqrt(jnp.mean(wide * wide, axis=-1, keepdims=True) + EPSILON)
+        rms_out[...] = rms_s[...]
+        acc_k[...] = jnp.zeros_like(acc_k)
+        acc_v[...] = jnp.zeros_like(acc_v)
+
+    normed = (tok_part[...].astype(jnp.float32) * rms_s[...] * gain[...]).astype(jnp.bfloat16)
+    normed_out[0] = normed
+    acc_k[...] += dot32(normed, wk[...])
+    acc_v[...] += dot32(normed, wv[...])
+
+    @pl.when(step == pl.num_programs(0) - 1)
+    def _():
+        kv_heads = acc_k.shape[1] // head
+        for group in range(kv_heads):
+            columns = slice(group * head, (group + 1) * head)
+            key_pre = acc_k[:, columns]
+            rotated = key_pre * cosine[...] - pltpu.roll(key_pre, head // 2, 1) * sine[...]
+            rotated = rotated.astype(jnp.bfloat16)
+            value = acc_v[:, columns].astype(jnp.bfloat16)
+            for seq in range(pairs // kv_heads):
+                rows = slice(seq * seq_rows, (seq + 1) * seq_rows)
+                kv_out[seq * kv_heads + group, :, :head] = rotated[rows]
+                kv_out[seq * kv_heads + group, :, head:] = value[rows]
+
+
+def attend_kernel(
+    query, grad, kv, cosine, sine, key_pos, query_pos, att_out, dq_out, pre_out, acc_k, acc_v
+):
+    step = pl.program_id(0)
+    head = query.shape[1]
+    scale = head ** (-0.5)
+
+    @pl.when(step == 0)
+    def _():
+        acc_k[...] = jnp.zeros_like(acc_k)
+        acc_v[...] = jnp.zeros_like(acc_v)
+
+    q = query[...]
+    g = grad[...]
+    k = kv[:, :head]
+    v = kv[:, head:]
+    grad_t = g.T
+    scores = lax.dot_general(k, q, NT, preferred_element_type=jnp.float32) * scale
+    scores = jnp.where(key_pos[...] <= query_pos[...], scores, -1e30)
+    exponent = jnp.exp(scores - jnp.max(scores, axis=0, keepdims=True))
+    prob = exponent * (1.0 / jnp.sum(exponent, axis=0, keepdims=True))
+    prob_b = prob.astype(jnp.bfloat16)
+    att_t = dot32(v.T, prob_b)
+    att_out[...] = att_t.T.astype(jnp.bfloat16)
+    att_r = att_t.astype(jnp.bfloat16).astype(jnp.float32)
+    delta = jnp.sum(att_r * grad_t.astype(jnp.float32), axis=0, keepdims=True)
+    dprob = dot32(v, grad_t)
+    dscores = (prob * (dprob - delta)).astype(jnp.bfloat16)
+    dq_out[...] = (dot32(k.T, dscores) * scale).T.astype(jnp.bfloat16)
+    acc_k[...] += dot32(dscores, q)
+    acc_v[...] += dot32(prob_b, g)
+
+    @pl.when(step == pl.num_programs(0) - 1)
+    def _():
+        key_grad = acc_k[...] * scale
+        back = key_grad * cosine[...] + pltpu.roll(key_grad, head // 2, 1) * sine[...]
+        pre_out[:, :head] = back.astype(jnp.bfloat16)
+        pre_out[:, head:] = acc_v[...].astype(jnp.bfloat16)
+
+
+def weight_kernel(normed_t, pre, out):
+    seqs, _, seq, _ = pre.shape
+    total = dot32(normed_t[:, :seq], pre[0, 0])
+    for s in range(1, seqs):
+        total += dot32(normed_t[:, s * seq : (s + 1) * seq], pre[s, 0])
+    out[...] = total.astype(jnp.bfloat16).reshape(out.shape)
+
+
+def token_kernel(place, pre, wk, wv, tok_all, tok_part, gain, gain_part, rms, out, pk, pv, ng, inner):
+    step = pl.program_id(0)
+    seqs, kv_heads, _, rows, pair_width = pre.shape
+    head = pair_width // 2
+
+    @pl.when(step == 0)
+    def _():
+        for s in range(seqs):
+            for h in range(kv_heads):
+                pk[s * rows : (s + 1) * rows, h * head : (h + 1) * head] = pre[s, h, 0, :, :head]
+                pv[s * rows : (s + 1) * rows, h * head : (h + 1) * head] = pre[s, h, 0, :, head:]
+        inner[...] = jnp.zeros_like(inner)
+
+    grad = lax.dot_general(pk[...], wk[...], NT, preferred_element_type=jnp.float32)
+    grad += lax.dot_general(pv[...], wv[...], NT, preferred_element_type=jnp.float32)
+    grad = grad * gain_part[...]
+    ng[step] = grad
+    inner[...] += jnp.sum(grad * tok_part[...].astype(jnp.float32), axis=-1, keepdims=True)
+
+    @pl.when(step == pl.num_programs(0) - 1)
+    def _():
+        scale = rms[...]
+        factor = scale * scale * scale * (inner[...] / tok_all.shape[1])
+        width = ng.shape[2]
+        for j in range(ng.shape[0]):
+            part = slice(j * width, (j + 1) * width)
+            wide = tok_all[:, part].astype(jnp.float32)
+            out[:, part] = (scale * ng[j] - wide * factor).astype(jnp.bfloat16)
+
+
+def last_kernel(place, parts, wk, wv, gk, gv, gain):
+    total = parts[0].astype(jnp.float32)
+    for i in range(1, parts.shape[0]):
+        total += parts[i].astype(jnp.float32)
+    kv_width = gk.shape[1]
+    head = HEAD_DIM
+    gain_sum = jnp.zeros((gk.shape[0], head), jnp.float32)
+    for h in range(kv_width // head):
+        columns = slice(h * head, (h + 1) * head)
+        key_part = total[:, 2 * h * head : (2 * h + 1) * head]
+        value_part = total[:, (2 * h + 1) * head : (2 * h + 2) * head]
+        gk[:, columns] = key_part
+        gv[:, columns] = value_part
+        gain_sum += key_part * wk[:, columns].astype(jnp.float32)
+        gain_sum += value_part * wv[:, columns].astype(jnp.float32)
+    gain[...] = jnp.sum(gain_sum, axis=-1, keepdims=True)
+
+
+def shape(dims, kind):
+    return jax.ShapeDtypeStruct(dims, kind)
+
+
+def whole_block(dims):
+    return pl.BlockSpec(dims, lambda *_: (0,) * len(dims))
+
+
+def exchange(values, axis):
+    return lax.all_to_all(values, axis, split_axis=0, concat_axis=0, tiled=True)
+
+
+def gather_ctx(values, count):
+    copies = jnp.broadcast_to(values[None], (count,) + values.shape)
+    return exchange(copies, "ctx")
+
+
+def body_heads(tokens, queries, d_attended, span_order, norm_gain, key_weight, value_weight):
+    bf16, f32 = jnp.bfloat16, jnp.float32
+    seqs, rows, width = tokens.shape
+    kv_width = key_weight.shape[1]
+    kv_heads = kv_width // HEAD_DIM
+    n_ctx = lax.axis_size("ctx")
+    n_dp = lax.axis_size("dp")
+    pairs = seqs * kv_heads
+    seq = rows * n_ctx
+    group_width = queries.shape[2] // kv_heads
+    heads = group_width // HEAD_DIM
+    part = width // n_ctx
+    all_rows = seqs * rows
+    pair_width = 2 * HEAD_DIM
+    place = lax.axis_index("ctx").astype(jnp.int32)
+    slot = (place * n_dp + lax.axis_index("dp").astype(jnp.int32)).reshape(1)
+
+    def to_pairs(x):
+        x = x.reshape(seqs, rows, kv_heads, group_width)
+        return jnp.transpose(x, (0, 2, 1, 3)).reshape(pairs, rows, group_width)
+
+    def from_pairs(x):
+        x = x.reshape(seqs, kv_heads, rows, group_width)
+        return jnp.transpose(x, (0, 2, 1, 3)).reshape(seqs, rows, kv_heads * group_width)
+
+    q_in = exchange(to_pairs(queries), "ctx").reshape(seq, group_width)
+    g_in = exchange(to_pairs(d_attended), "ctx").reshape(seq, group_width)
+
+    token_pos = positions(span_order, rows // 2)
+    cosine, sine = rotation(token_pos, HEAD_DIM)
+    sign = jnp.where(jnp.arange(HEAD_DIM) < HEAD_DIM // 2, 1.0, -1.0).astype(f32)
+    sine = sine * sign[None, :]
+    own_cos = jnp.tile(lax.dynamic_slice_in_dim(cosine, place * rows, rows, 0), (seqs, 1))
+    own_sin = jnp.tile(lax.dynamic_slice_in_dim(sine, place * rows, rows, 0), (seqs, 1))
+    flat = tokens.reshape(all_rows, width)
+    gain_row = norm_gain[None, :]
+
+    normed, rms, kv = pl.pallas_call(
+        project_kernel,
+        grid=(n_ctx,),
+        in_specs=[
+            whole_block((all_rows, width)),
+            pl.BlockSpec((all_rows, part), lambda j: (0, j)),
+            pl.BlockSpec((1, part), lambda j: (0, j)),
+            pl.BlockSpec((part, kv_width), lambda j: (j, 0)),
+            pl.BlockSpec((part, kv_width), lambda j: (j, 0)),
+            whole_block((all_rows, HEAD_DIM)),
+            whole_block((all_rows, HEAD_DIM)),
+        ],
+        out_specs=[
+            pl.BlockSpec((1, all_rows, part), lambda j: (j, 0, 0)),
+            whole_block((all_rows, 1)),
+            whole_block((pairs, rows, pair_width)),
+        ],
+        out_shape=[
+            shape((n_ctx, all_rows, part), bf16),
+            shape((all_rows, 1), f32),
+            shape((pairs, rows, pair_width), bf16),
+        ],
+        scratch_shapes=[
+            pltpu.VMEM((all_rows, kv_width), f32),
+            pltpu.VMEM((all_rows, kv_width), f32),
+            pltpu.VMEM((all_rows, 1), f32),
+        ],
+        name="project",
+    )(flat, flat, gain_row, key_weight, value_weight, own_cos, own_sin)
+
+    kv_in = exchange(kv, "ctx").reshape(seq, pair_width)
+    normed_in = exchange(normed, "ctx").reshape(n_ctx, seqs, rows, part)
+    normed_t = jnp.transpose(normed_in, (3, 1, 0, 2)).reshape(part, seqs * seq)
+
+    attended, dquery, pre = pl.pallas_call(
+        attend_kernel,
+        grid=(heads,),
+        in_specs=[
+            pl.BlockSpec((seq, HEAD_DIM), lambda h: (0, h)),
+            pl.BlockSpec((seq, HEAD_DIM), lambda h: (0, h)),
+            whole_block((seq, pair_width)),
+            whole_block((seq, HEAD_DIM)),
+            whole_block((seq, HEAD_DIM)),
+            whole_block((seq, 1)),
+            whole_block((1, seq)),
+        ],
+        out_specs=[
+            pl.BlockSpec((seq, HEAD_DIM), lambda h: (0, h)),
+            pl.BlockSpec((seq, HEAD_DIM), lambda h: (0, h)),
+            whole_block((seq, pair_width)),
+        ],
+        out_shape=[
+            shape((seq, group_width), bf16),
+            shape((seq, group_width), bf16),
+            shape((seq, pair_width), bf16),
+        ],
+        scratch_shapes=[pltpu.VMEM((seq, HEAD_DIM), f32), pltpu.VMEM((seq, HEAD_DIM), f32)],
+        name="attend",
+    )(q_in, g_in, kv_in, cosine, sine, token_pos[:, None], token_pos[None, :])
+
+    pre_all = gather_ctx(pre, n_ctx).reshape(seqs, kv_heads, seq, pair_width)
+
+    weight_parts = pl.pallas_call(
+        weight_kernel,
+        grid=(kv_heads,),
+        in_specs=[
+            whole_block((part, seqs * seq)),
+            pl.BlockSpec((seqs, 1, seq, pair_width), lambda h: (0, h, 0, 0)),
+        ],
+        out_specs=pl.BlockSpec((n_dp, part // n_dp, pair_width), lambda h: (0, 0, h)),
+        out_shape=shape((n_dp, part // n_dp, 2 * kv_width), bf16),
+        name="weights",
+    )(normed_t, pre_all)
+    weight_in = exchange(weight_parts, "dp")
+
+    att_back = from_pairs(exchange(attended.reshape(n_ctx, rows, group_width), "ctx"))
+    dq_back = from_pairs(exchange(dquery.reshape(n_ctx, rows, group_width), "ctx"))
+
+    grad_tokens = pl.pallas_call(
+        token_kernel,
+        grid_spec=pltpu.PrefetchScalarGridSpec(
+            num_scalar_prefetch=1,
+            grid=(n_ctx,),
+            in_specs=[
+                pl.BlockSpec((seqs, kv_heads, 1, rows, pair_width), lambda j, p: (0, 0, p[0], 0, 0)),
+                pl.BlockSpec((part, kv_width), lambda j, p: (j, 0)),
+                pl.BlockSpec((part, kv_width), lambda j, p: (j, 0)),
+                whole_block((all_rows, width)),
+                pl.BlockSpec((all_rows, part), lambda j, p: (0, j)),
+                whole_block((1, width)),
+                pl.BlockSpec((1, part), lambda j, p: (0, j)),
+                whole_block((all_rows, 1)),
+            ],
+            out_specs=whole_block((all_rows, width)),
+            scratch_shapes=[
+                pltpu.VMEM((all_rows, kv_width), bf16),
+                pltpu.VMEM((all_rows, kv_width), bf16),
+                pltpu.VMEM((n_ctx, all_rows, part), f32),
+                pltpu.VMEM((all_rows, 1), f32),
+            ],
+        ),
+        out_shape=shape((all_rows, width), bf16),
+        name="tokens",
+    )(
+        place.reshape(1),
+        pre_all.reshape(seqs, kv_heads, n_ctx, rows, pair_width),
+        key_weight,
+        value_weight,
+        flat,
+        flat,
+        gain_row,
+        gain_row,
+        rms,
+    )
+
+    own = part // n_dp
+    grad_key, grad_value, gain_sum = pl.pallas_call(
+        last_kernel,
+        grid_spec=pltpu.PrefetchScalarGridSpec(
+            num_scalar_prefetch=1,
+            grid=(1,),
+            in_specs=[
+                whole_block((n_dp, own, 2 * kv_width)),
+                pl.BlockSpec((own, kv_width), lambda j, p: (p[0], 0)),
+                pl.BlockSpec((own, kv_width), lambda j, p: (p[0], 0)),
+            ],
+            out_specs=[
+                whole_block((own, kv_width)),
+                whole_block((own, kv_width)),
+                whole_block((own, 1)),
+            ],
+        ),
+        out_shape=[shape((own, kv_width), f32), shape((own, kv_width), f32), shape((own, 1), f32)],
+        name="last",
+    )(slot, weight_in, key_weight, value_weight)
+    own_gain = lax.dynamic_slice_in_dim(norm_gain, slot[0] * own, own, 0)
+    grad_gain = gain_sum[:, 0] / own_gain
+    return (
+        att_back,
+        dq_back,
+        grad_tokens.reshape(seqs, rows, width),
+        grad_key,
+        grad_value,
+        grad_gain,
+    )
+
+
+def body(tokens, queries, d_attended, span_order, norm_gain, key_weight, value_weight):
+    pairs = tokens.shape[0] * (key_weight.shape[1] // HEAD_DIM)
+    chosen = body_heads if pairs == lax.axis_size("ctx") else body_rows
+    return chosen(tokens, queries, d_attended, span_order, norm_gain, key_weight, value_weight)
+
+
 def solution(mesh):
     placed = (P("dp", "ctx", None), P("dp", "ctx", None), P("dp", "ctx", None), P(), P(), P(), P())
     return jax.shard_map(

time: 514 us -> 216 us (0.42)
  waiting for transfers between devices: 344 us -> 43.1 us
  matrix products: 75.4 us -> 0 us
  blocking collectives: 27.4 us -> 98.6 us
  Pallas kernels: 0 us -> 34.3 us
  starting transfers between devices: 0.69 us -> 21.6 us
  between operations: 17.6 us -> 0.79 us
  other arithmetic: 21.8 us -> 5.9 us
  local copies, waits for them, and re-layouts: 26.2 us -> 10.6 us
    reduce_scatter x4 -> x0, waiting for transfers between devices: 171 us -> none  [the longest x1 68.7 us: body(): lax.psum_scatter(weight_key.astype(jnp.bfloat16), 'ctx', scatter_dimensio...]
    unnamed x8 -> x0, waiting for transfers between devices: 99.4 us -> none
    all_to_all x0 -> x3, blocking collectives: none -> 98.6 us  [exchange(): return lax.all_to_all(values, axis, split_axis=0, concat_axis=0, tiled=True)]
    all_gather x2 -> x0, waiting for transfers between devices: 72.7 us -> none  [the longest x1 36.9 us: body(): lax.all_gather(rotated_keys, 'ctx', axis=1, tiled=True)]
    dot_general x46 -> x0, matrix products: 58 us -> none  [the longest x8 14.3 us: attend_group(): jnp.einsum('gts,sd->tgd', probability_b, value_group, preferred_element_t...]
    all_to_all x0 -> x5, waiting for transfers between devices: none -> 43.1 us  [exchange(): return lax.all_to_all(values, axis, split_axis=0, concat_axis=0, tiled=True)]
    pallas_call x0 -> x5, Pallas kernels: none -> 34.3 us  [the longest x1 10.1 us: body_heads(): pl.pallas_call(token_kernel, grid_spec=pltpu.PrefetchScalarGridSpec(num_s...]
    unnamed x2 -> x0, blocking collectives: 27.4 us -> none
  transfers between devices with their start and end apart: 7 -> 5, of which waited for: 7 -> 5; matrix products, arithmetic and copies ran while one was open for 8% -> 4% of each run, Pallas kernels for 0% -> 7%
where the time goes in v1:
time: 216 us; the launch traced here: 215 us
  blocking collectives  98.6 us (46%)
  waiting for transfers between devices  43.1 us (20%)
  Pallas kernels  34.3 us (16%)
  starting transfers between devices  21.6 us (10%)
  local copies, waits for them, and re-layouts  10.6 us (5%)
  other arithmetic  5.9 us (3%)
    all_to_all x3, blocking collectives, exchange(): return lax.all_to_all(values, axis, split_axis=0, concat_axis=0, tiled=True)  98.6 us
    all_to_all x5, waiting for transfers between devices, exchange(): return lax.all_to_all(values, axis, split_axis=0, concat_axis=0, tiled=True)  43.1 us
    all_to_all x5, starting transfers between devices, exchange(): return lax.all_to_all(values, axis, split_axis=0, concat_axis=0, tiled=True)  21.6 us
    pallas_call x1, Pallas kernels, body_heads(): pl.pallas_call(token_kernel, grid_spec=pltpu.PrefetchScalarGridSpec(num_s...  10.1 us
    pallas_call x1, Pallas kernels, body_heads(): pl.pallas_call(project_kernel, grid=(n_ctx,), in_specs=[whole_block((all_...  9.29 us
    pallas_call x1, Pallas kernels, body_heads(): pl.pallas_call(attend_kernel, grid=(heads,), in_specs=[pl.BlockSpec((seq,...  7.82 us
    pallas_call x1, Pallas kernels, body_heads(): pl.pallas_call(weight_kernel, grid=(kv_heads,), in_specs=[whole_block((pa...  4.81 us
  transfers between devices with their start and end apart: 5, of which 5 were waited for; matrix products, arithmetic and copies ran while one was open for 4% of the time, Pallas kernels for 7%

profile of v1, /device:TPU:0, one launch (start us, length us, event | category | flops | bytes accessed | tf_op | source)
XLA Modules:
  0.0 214.8 jit_solution(1325461942210490117)
XLA Ops:
  0.7 0.7 broadcast_multiply_fusion.1
  1.6 1.1 sine_multiply_fusion
  2.8 0.7 tile.8
  4.2 9.3 %project.1 = (bf16[8,128,512]{2,1,0:T(8,128)(2,1)}, f32[128,1]{1,0:T(8,128)}, bf16[8,64,256]{2,1,0:T(8,128)(2,1)}) custom-call(bf16[128,4096]{1,0:T(8,128)(2,1)} %bitcast.30, bf16[128,4096]{1,0:T(8,128)(2,1)} %bitcast.31, f32[1,4096]{1,0:T(1,128)} %bitcast.47, bf16[4096,512]{1,0:T(8,128)(2,1)} %wk.5, bf16[4096,512]{1,0:T(8,128)(2,1)} %wv.5, ...), custom_call_target="tpu_custom_call" | custom-call | tf_op jit(solution)/shard_map/project/pallas_call | solution.py:440
  13.5 7.3 %all-to-all-start.2 = ((bf16[8,64,256]{2,1,0:T(8,128)(2,1)}), bf16[8,64,256]{2,1,0:T(8,128)(2,1)S(1)}, u32[]{:S(2)}, u32[]{:S(2)}) async-start(bf16[8,64,256]{2,1,0:T(8,128)(2,1)} %get-tuple-element.15), calls=%async_computation.2 | async-start | bytes 524288 | tf_op jit(solution)/shard_map/all_to_all | solution.py:395
  20.9 0.8 pad_maximum_fusion
  21.7 8.0 %all-to-all-done.2 = bf16[8,64,256]{2,1,0:T(8,128)(2,1)S(1)} async-done(((bf16[8,64,256]{2,1,0:T(8,128)(2,1)}), bf16[8,64,256]{2,1,0:T(8,128)(2,1)S(1)}, u32[]{:S(2)}, u32[]{:S(2)}) %all-to-all-start.2) | async-done | bytes 262176 | tf_op jit(solution)/shard_map/all_to_all | solution.py:395
  29.7 3.6 %all-to-all-start = ((bf16[8,64,512]{2,1,0:T(8,128)(2,1)}), bf16[8,64,512]{2,1,0:T(8,128)(2,1)S(1)}, u32[]{:S(2)}, u32[]{:S(2)}) async-start(bf16[8,64,512]{2,1,0:T(8,128)(2,1)} %bitcast), calls=%async_computation | async-start | bytes 1048576 | tf_op jit(solution)/shard_map/all_to_all | solution.py:395
  33.4 0.8 pad_maximum_fusion.1
  34.2 13.3 %all-to-all-done = bf16[8,64,512]{2,1,0:T(8,128)(2,1)S(1)} async-done(((bf16[8,64,512]{2,1,0:T(8,128)(2,1)}), bf16[8,64,512]{2,1,0:T(8,128)(2,1)S(1)}, u32[]{:S(2)}, u32[]{:S(2)}) %all-to-all-start) | async-done | bytes 524320 | tf_op jit(solution)/shard_map/all_to_all | solution.py:395
  47.5 3.6 %all-to-all-start.1 = ((bf16[8,64,512]{2,1,0:T(8,128)(2,1)}), bf16[8,64,512]{2,1,0:T(8,128)(2,1)S(1)}, u32[]{:S(2)}, u32[]{:S(2)}) async-start(bf16[8,64,512]{2,1,0:T(8,128)(2,1)} %bitcast.2), calls=%async_computation.1 | async-start | bytes 1048576 | tf_op jit(solution)/shard_map/all_to_all | solution.py:395
  51.1 1.0 add.56.key_pos
  52.7 12.8 %all-to-all-done.1 = bf16[8,64,512]{2,1,0:T(8,128)(2,1)S(1)} async-done(((bf16[8,64,512]{2,1,0:T(8,128)(2,1)}), bf16[8,64,512]{2,1,0:T(8,128)(2,1)S(1)}, u32[]{:S(2)}, u32[]{:S(2)}) %all-to-all-start.1) | async-done | bytes 524320 | tf_op jit(solution)/shard_map/all_to_all | solution.py:395
  65.5 0.8 copy-done.2
  66.3 7.8 %attend.1 = (bf16[512,512]{1,0:T(8,128)(2,1)}, bf16[512,512]{1,0:T(8,128)(2,1)}, bf16[512,256]{1,0:T(8,128)(2,1)}) custom-call(bf16[512,512]{1,0:T(8,128)(2,1)} %bitcast.36, bf16[512,512]{1,0:T(8,128)(2,1)} %bitcast.37, bf16[512,256]{1,0:T(8,128)(2,1)} %bitcast.42, f32[512,128]{1,0:T(8,128)} %copy-done.4, f32[512,128]{1,0:T(8,128)} %copy-done.3, ...), custom_call_target="tpu_custom_call" | custom-call | tf_op jit(solution)/shard_map/attend/pallas_call | solution.py:474
  74.2 18.3 %all_to_all.40 = bf16[8,64,512]{2,1,0:T(8,128)(2,1)S(1)} all-to-all(bf16[8,64,512]{2,1,0:T(8,128)(2,1)} %bitcast.44), channel_id=1, replica_groups=mesh['ctx'=8,'dp'=4] {'ctx'}, dimensions={0} | all-to-all | bytes 1048576 | tf_op jit(solution)/shard_map/all_to_all | solution.py:395
  92.5 28.9 %all_to_all.41 = bf16[8,128,512]{2,1,0:T(8,128)(2,1)S(1)} all-to-all(bf16[8,128,512]{2,1,0:T(8,128)(2,1)S(1)} %copy-done.6), channel_id=1, replica_groups=mesh['ctx'=8,'dp'=4] {'ctx'}, dimensions={0} | all-to-all | bytes 2097152 | tf_op jit(solution)/shard_map/all_to_all | solution.py:395
  121.4 1.1 broadcast_in_dim.25
  122.5 51.4 %all_to_all.42 = bf16[8,512,256]{2,1,0:T(8,128)(2,1)} all-to-all(bf16[8,512,256]{2,1,0:T(8,128)(2,1)S(1)} %broadcast_in_dim.25), channel_id=1, replica_groups=mesh['ctx'=8,'dp'=4] {'ctx'}, dimensions={0} | all-to-all | bytes 4194304 | tf_op jit(solution)/shard_map/all_to_all | solution.py:395
  173.8 3.5 %all-to-all-start.4 = ((bf16[8,64,512]{2,1,0:T(8,128)(2,1)}), bf16[8,64,512]{2,1,0:T(8,128)(2,1)S(1)}, u32[]{:S(2)}, u32[]{:S(2)}) async-start(bf16[8,64,512]{2,1,0:T(8,128)(2,1)} %bitcast.12), calls=%async_computation.4 | async-start | bytes 1048576 | tf_op jit(solution)/shard_map/all_to_all | solution.py:395
  177.4 1.3 copy.20.normed_t
  178.7 4.8 %weights.1 = bf16[4,128,1024]{2,1,0:T(8,128)(2,1)} custom-call(bf16[512,1024]{1,0:T(8,128)(2,1)} %copy.20.normed_t, bf16[2,4,512,256]{3,2,1,0:T(8,128)(2,1)} %bitcast.28), custom_call_target="tpu_custom_call" | custom-call | tf_op jit(solution)/shard_map/weights/pallas_call | solution.py:502
  183.5 7.9 %all-to-all-done.4 = bf16[8,64,512]{2,1,0:T(8,128)(2,1)S(1)} async-done(((bf16[8,64,512]{2,1,0:T(8,128)(2,1)}), bf16[8,64,512]{2,1,0:T(8,128)(2,1)S(1)}, u32[]{:S(2)}, u32[]{:S(2)}) %all-to-all-start.4) | async-done | bytes 524320 | tf_op jit(solution)/shard_map/all_to_all | solution.py:395
  191.4 3.5 %all-to-all-start.7 = ((bf16[4,128,1024]{2,1,0:T(8,128)(2,1)}), bf16[4,128,1024]{2,1,0:T(8,128)(2,1)S(1)}, u32[]{:S(2)}, u32[]{:S(2)}) async-start(bf16[4,128,1024]{2,1,0:T(8,128)(2,1)} %weights.1), calls=%async_computation.7 | async-start | bytes 2097152 | tf_op jit(solution)/shard_map/all_to_all | solution.py:395
  195.4 1.2 reshape.153
  196.9 1.2 reshape.156
  198.1 10.1 %tokens.1 = bf16[128,4096]{1,0:T(8,128)(2,1)} custom-call(s32[1]{0:T(128)} %bitcast.15.place, bf16[2,4,8,64,256]{4,3,2,1,0:T(8,128)(2,1)} %bitcast.29, bf16[4096,512]{1,0:T(8,128)(2,1)} %wk.5, bf16[4096,512]{1,0:T(8,128)(2,1)} %wv.5, bf16[128,4096]{1,0:T(8,128)(2,1)} %bitcast.32, bf16[128,4096]{1,0:T(8,128)(2,1)} %bitcast.33, f32[1,4096]{1,0:T(1,128)} %bitcast.48, ...), custom_call_target="tpu_custom_call" | custom-call | tf_op jit(solution)/shard_map/tokens/pallas_call | solution.py:518
  208.2 1.1 all-to-all-done.7.parts
  209.3 1.0 copy-done
  210.3 2.3 %last.1 = (f32[128,512]{1,0:T(8,128)}, f32[128,512]{1,0:T(8,128)}, f32[128,1]{1,0:T(8,128)}) custom-call(s32[1]{0:T(128)} %bitcast.18.place, bf16[4,128,1024]{2,1,0:T(8,128)(2,1)} %copy-done, bf16[4096,512]{1,0:T(8,128)(2,1)} %wk.5, bf16[4096,512]{1,0:T(8,128)(2,1)} %wv.5), custom_call_target="tpu_custom_call" | custom-call | tf_op jit(solution)/shard_map/last/pallas_call | solution.py:556
  212.6 0.9 reduce
  213.5 1.3 dynamic-slice_divide_fusion
  (29 shorter events, 2.6 us)
Async XLA Ops:
  2.8 10.7 %copy-start.3 = (f32[512,128]{1,0:T(8,128)}, f32[512,128]{1,0:T(8,128)S(1)}, u32[]{:S(2)}) copy-start(f32[512,128]{1,0:T(8,128)S(1)} %get-tuple-element.32.sine) | copy-start | bytes 786436
  2.8 10.7 %copy-start.4 = (f32[512,128]{1,0:T(8,128)}, f32[512,128]{1,0:T(8,128)S(1)}, u32[]{:S(2)}) copy-start(f32[512,128]{1,0:T(8,128)S(1)} %get-tuple-element.33.cosine) | copy-start | bytes 786436
  4.2 16.6 %copy-start.7 = (bf16[2,64,2048]{2,1,0:T(8,128)(2,1)S(1)}, bf16[2,64,2048]{2,1,0:T(8,128)(2,1)}, u32[]{:S(2)}) copy-start(bf16[2,64,2048]{2,1,0:T(8,128)(2,1)} %param.8) | copy-start | bytes 1572868
  4.2 29.1 %copy-start.8 = (bf16[2,64,2048]{2,1,0:T(8,128)(2,1)S(1)}, bf16[2,64,2048]{2,1,0:T(8,128)(2,1)}, u32[]{:S(2)}) copy-start(bf16[2,64,2048]{2,1,0:T(8,128)(2,1)} %param.9) | copy-start | bytes 1572868
  13.5 16.2 %all-to-all-start.2 = ((bf16[8,64,256]{2,1,0:T(8,128)(2,1)}), bf16[8,64,256]{2,1,0:T(8,128)(2,1)S(1)}, u32[]{:S(2)}, u32[]{:S(2)}) async-start(bf16[8,64,256]{2,1,0:T(8,128)(2,1)} %get-tuple-element.15), calls=%async_computation.2 | async-start | bytes 524288 | tf_op jit(solution)/shard_map/all_to_all | solution.py:395
  20.8 71.6 %copy-start.6 = (bf16[8,128,512]{2,1,0:T(8,128)(2,1)S(1)}, bf16[8,128,512]{2,1,0:T(8,128)(2,1)}, u32[]{:S(2)}) copy-start(bf16[8,128,512]{2,1,0:T(8,128)(2,1)} %get-tuple-element.20) | copy-start | bytes 3145732
  29.7 35.8 %copy-start.5 = (bf16[8,64,256]{2,1,0:T(8,128)(2,1)}, bf16[8,64,256]{2,1,0:T(8,128)(2,1)S(1)}, u32[]{:S(2)}) copy-start(bf16[8,64,256]{2,1,0:T(8,128)(2,1)S(1)} %all-to-all-done.2) | copy-start | bytes 786436
  29.7 17.8 %all-to-all-start = ((bf16[8,64,512]{2,1,0:T(8,128)(2,1)}), bf16[8,64,512]{2,1,0:T(8,128)(2,1)S(1)}, u32[]{:S(2)}, u32[]{:S(2)}) async-start(bf16[8,64,512]{2,1,0:T(8,128)(2,1)} %bitcast), calls=%async_computation | async-start | bytes 1048576 | tf_op jit(solution)/shard_map/all_to_all | solution.py:395
  47.5 18.1 %copy-start.1 = (bf16[8,64,512]{2,1,0:T(8,128)(2,1)}, bf16[8,64,512]{2,1,0:T(8,128)(2,1)S(1)}, u32[]{:S(2)}) copy-start(bf16[8,64,512]{2,1,0:T(8,128)(2,1)S(1)} %all-to-all-done) | copy-start | bytes 1572868
  47.5 18.1 %all-to-all-start.1 = ((bf16[8,64,512]{2,1,0:T(8,128)(2,1)}), bf16[8,64,512]{2,1,0:T(8,128)(2,1)S(1)}, u32[]{:S(2)}, u32[]{:S(2)}) async-start(bf16[8,64,512]{2,1,0:T(8,128)(2,1)} %bitcast.2), calls=%async_computation.1 | async-start | bytes 1048576 | tf_op jit(solution)/shard_map/all_to_all | solution.py:395
  65.5 0.8 copy-start.2
  173.8 17.6 %all-to-all-start.4 = ((bf16[8,64,512]{2,1,0:T(8,128)(2,1)}), bf16[8,64,512]{2,1,0:T(8,128)(2,1)S(1)}, u32[]{:S(2)}, u32[]{:S(2)}) async-start(bf16[8,64,512]{2,1,0:T(8,128)(2,1)} %bitcast.12), calls=%async_computation.4 | async-start | bytes 1048576 | tf_op jit(solution)/shard_map/all_to_all | solution.py:395
  191.4 17.9 %all-to-all-start.7 = ((bf16[4,128,1024]{2,1,0:T(8,128)(2,1)}), bf16[4,128,1024]{2,1,0:T(8,128)(2,1)S(1)}, u32[]{:S(2)}, u32[]{:S(2)}) async-start(bf16[4,128,1024]{2,1,0:T(8,128)(2,1)} %weights.1), calls=%async_computation.7 | async-start | bytes 2097152 | tf_op jit(solution)/shard_map/all_to_all | solution.py:395
  209.3 1.0 copy-start
